TPU v7x, 32 devices: a whole 2x2x4 slice. The times are simulated.
32 devices in a mesh: slab: 4 (over y, core), bl: 8 (over z, x).
Axes of the slice: x: 2, y: 2, z: 4, core: 2. Of those that a mesh axis runs over, the one named last changes fastest.
Arguments:
- model_image: float32 [2, 8192, 8192], P(None, 'slab', 'bl'), may hold values from -6 to 6
- vis_coords: float32 [512, 2, 128], P(('slab', 'bl')), may hold values from 0 to 32
- vis_observed: float32 [512, 2, 128], P(('slab', 'bl')), may hold values from -6 to 6
- tile_slot: int32 [512], P(('slab', 'bl')), may hold values from 0 to 2047
- tile_group: int32 [512, 1], P(('slab', 'bl')), may hold values from 0 to 7; in each aligned block of 16 rows (0 to 15, 16 to 31, ...) at most 8 rows name the same one
- w_plane: int32 [512], P(('slab', 'bl')), may hold values from 0 to 7
- vis_count: int32 [512], P(('slab', 'bl')), may hold values from 16 to 128, as said below
Outputs:
- residual_image: float32 [2, 8192, 8192], P(None, 'slab', 'bl')
- residual_vis: float32 [512, 2, 128], P(('slab', 'bl'))
Inputs may be any that keep to these rules, and one draw needn't show every extreme that they name: `tile_group`: among the 16 subgrids of one device, at most 8 name the same group. `vis_count`: some subgrid holds exactly 128 visibilities.
All inputs are finite; a program needn't handle non-finite values.
Results may differ from a plain program's by a relative error of at most 0.0003.
Values sent between devices are 32-bit elements; how exact they have to be, the bound alone decides.
No kernel may reach another device: no remote copies, remote signals or barrier semaphores. Data moves between devices by JAX's collectives and lax.ppermute only.
A program may use at most 192 MiB of HBM per device.

v0:
```python
import math
import jax
import jax.numpy as jnp
from jax import lax
from jax.sharding import PartitionSpec as P

SUB = 32
w_step = 0.1


def complex_einsum(form, left, right):
    product = lambda first, second: jnp.einsum(form, first, second, precision=lax.Precision.HIGHEST)
    return (
        product(left[0], right[0]) - product(left[1], right[1]),
        product(left[0], right[1]) + product(left[1], right[0]),
    )


def complex_mul(left, right):
    return (left[0] * right[0] - left[1] * right[1], left[0] * right[1] + left[1] * right[0])


def subgrid_pass(tile_real, tile_imag, coords, observed, planes, counts):
    width = tile_real.shape[-1]
    half = width // 2
    slots = coords.shape[-1]
    index = jnp.arange(width, dtype=jnp.int32)
    offsets = (index - half).astype(jnp.float32)
    turns = index[:, None] * (index[None, :] - half) % width
    angle = 2.0 * math.pi / width * turns.astype(jnp.float32)
    forward_d = (jnp.cos(angle), jnp.sin(angle))
    backward_d = (forward_d[0], -forward_d[1])
    scale_sub = 1.0 / (width * width)
    halfway = complex_einsum("il,kij->klj", forward_d, (tile_real, tile_imag))
    image_sub = complex_einsum("klj,jm->klm", halfway, forward_d)
    image_sub = (image_sub[0] * scale_sub, image_sub[1] * scale_sub)
    radius = (offsets[:, None] ** 2 + offsets[None, :] ** 2) / (half * half)
    phase = -w_step * planes.astype(jnp.float32)[:, None, None] * radius[None]
    screen = (jnp.cos(phase), jnp.sin(phase))
    weighted = complex_mul(screen, image_sub)
    along_a = -2.0 * math.pi / width * coords[:, 0, :][:, None, :] * offsets[None, :, None]
    along_b = -2.0 * math.pi / width * coords[:, 1, :][:, None, :] * offsets[None, :, None]
    phase_a = (jnp.cos(along_a), jnp.sin(along_a))
    phase_b = (jnp.cos(along_b), jnp.sin(along_b))
    partial_rows = complex_einsum("klm,kmj->klj", weighted, phase_b)
    terms = complex_mul(phase_a, partial_rows)
    predicted = (jnp.sum(terms[0], axis=1), jnp.sum(terms[1], axis=1))
    live = (jnp.arange(slots, dtype=jnp.int32)[None, :] < counts[:, None]).astype(jnp.float32)
    resid_real = (observed[:, 0, :] - predicted[0]) * live
    resid_imag = (observed[:, 1, :] - predicted[1]) * live
    spread = complex_mul(
        (phase_a[0], -phase_a[1]), (resid_real[:, None, :], resid_imag[:, None, :])
    )
    collected = complex_einsum("klj,kmj->klm", spread, (phase_b[0], -phase_b[1]))
    unscreened = complex_mul((screen[0], -screen[1]), collected)
    middle = complex_einsum("il,klm->kim", backward_d, unscreened)
    tile_out = complex_einsum("kim,jm->kij", middle, backward_d)
    return (
        jnp.stack([resid_real, resid_imag], axis=1),
        jnp.stack([tile_out[0] * scale_sub, tile_out[1] * scale_sub], axis=1),
    )


def table(product, modulus, sign):
    angle = 2.0 * math.pi / modulus * (product % modulus).astype(jnp.float32)
    return (jnp.cos(angle), sign * jnp.sin(angle))


def real_form(pair):
    return jnp.stack(
        [jnp.stack([pair[0], -pair[1]], axis=1), jnp.stack([pair[1], pair[0]], axis=1)], axis=0
    )


def product_high(form, left, right):
    return jnp.einsum(form, left, right, precision=lax.Precision.HIGH)


def twist(pair, values):
    return jnp.stack(complex_mul(pair, (values[0], values[1])))


def per_device(model_image, vis_coords, vis_observed, tile_slot, tile_group, w_plane, vis_count):
    groups = lax.axis_size("bl")
    bands = lax.axis_size("slab")
    both = ("slab", "bl")
    width_in = model_image.shape[2]
    extent = model_image.shape[1] * bands
    tile_rows = extent // SUB
    owned_cols = tile_rows // (groups * bands)
    sub_count = tile_slot.shape[0]
    tile_u = tile_slot % tile_rows
    tile_v = (
        lax.axis_index("slab") * groups + tile_group[:, 0]
    ) * owned_cols + tile_slot // tile_rows
    ids = lax.all_gather(tile_u * tile_rows + tile_v, both, axis=0, tiled=True)
    all_u = ids // tile_rows
    all_v = ids % tile_rows
    image = lax.all_to_all(model_image, "slab", split_axis=2, concat_axis=1, tiled=True)
    cols = image.shape[2]
    col = (
        lax.axis_index("bl") * width_in
        + lax.axis_index("slab") * cols
        + jnp.arange(cols, dtype=jnp.int32)
    )
    short = jnp.arange(SUB, dtype=jnp.int32)
    long = jnp.arange(tile_rows, dtype=jnp.int32)
    coarse = table(short[:, None] * short[None, :], SUB, -1.0)
    fine = table(short[:, None] * long[None, :], extent, -1.0)
    pick_u = table(all_u[:, None] * long[None, :], tile_rows, -1.0)
    shift_v = table(all_v[:, None] * col[None, :], tile_rows, -1.0)
    inside_v = table(short[:, None] * col[None, :], extent, -1.0)
    conj = lambda pair: (pair[0], -pair[1])
    lift_fine = lambda pair: (pair[0][:, :, None], pair[1][:, :, None])
    lift_v = lambda pair: (pair[0][:, None, :], pair[1][:, None, :])
    stage = product_high(
        "aibq,bqpc->aipc", real_form(coarse), image.reshape(2, SUB, tile_rows, cols)
    )
    stage = twist(lift_fine(fine), stage)
    strips = product_high("agbp,bipc->agic", real_form(pick_u), stage)
    strips = twist(lift_v(shift_v), strips)
    partial = product_high("ajbc,bgic->gaij", real_form(inside_v), strips) / extent
    mine = lax.psum_scatter(
        partial.reshape(-1, 2 * SUB * SUB), both, scatter_dimension=0, tiled=True
    )
    mine = mine.reshape(sub_count, 2, SUB, SUB)
    residual_vis, contrib = subgrid_pass(
        mine[:, 0], mine[:, 1], vis_coords, vis_observed, w_plane, vis_count
    )
    every = lax.all_gather(contrib.reshape(sub_count, 2 * SUB * SUB), both, axis=0, tiled=True)
    every = every.reshape(-1, 2, SUB, SUB)
    spread = product_high("ajbc,gaij->bgic", real_form(inside_v), every)
    spread = twist(lift_v(conj(shift_v)), spread)
    back = product_high("agbp,agic->bipc", real_form(pick_u), spread)
    back = twist(lift_fine(conj(fine)), back) / extent
    rows = product_high("aibq,aipc->bqpc", real_form(coarse), back)
    residual_image = lax.all_to_all(
        rows.reshape(2, extent, cols), "slab", split_axis=1, concat_axis=2, tiled=True
    )
    return (residual_image, residual_vis)


def solution(mesh):
    placed = (
        P(None, "slab", "bl"),
        P(("slab", "bl"), None, None),
        P(("slab", "bl"), None, None),
        P(("slab", "bl")),
        P(("slab", "bl"), None),
        P(("slab", "bl")),
        P(("slab", "bl")),
    )
    return jax.shard_map(
        per_device,
        mesh=mesh,
        in_specs=placed,
        out_specs=(P(None, "slab", "bl"), P(("slab", "bl"), None, None)),
        check_vma=False,
    )
```

profile of v0, /device:TPU:0, one launch (start us, length us, event | category | flops | bytes accessed | tf_op | source)
XLA Modules:
  0.0 1117.9 jit_solution(155449338450149249)
XLA Ops:
  7.2 25.3 %copy.94 = f32[2,2048,1024]{1,0,2:T(2,128)} copy(f32[2,2048,1024]{2,1,0:T(8,128)} %param.7) | data formatting | bytes 33554432 | tf_op args[0]
  32.5 7.1 all-to-all-start
  39.8 218.7 %all-reduce = s32[512]{0:T(512)S(1)} all-reduce(s32[512]{0:T(512)S(1)} %fusion.206), channel_id=1, replica_groups=mesh['slab'=4,'bl'=8] {'slab','bl'}, use_global_device_ids=true, to_apply=%add | all-reduce | flops 512 | bytes 4096
  258.8 1.2 sine_multiply_fusion.2
  260.1 2.1 fusion.95
  262.4 3.2 fusion.96
  265.5 17.7 %copy.95 = f32[2,2048,1024]{1,2,0:T(8,128)} copy(f32[2,2048,1024]{1,0,2:T(2,128)} %all-to-all-done) | data formatting | bytes 33554432 | tf_op jit(solution)/shard_map/all_to_all | solution.py:99
  283.3 16.5 %copy.96 = f32[2,4,2048,256]{3,2,1,0:T(8,128)} copy(f32[2,4,2048,256]{2,3,1,0:T(8,128)} %bitcast.175) | data formatting | bytes 33554432 | tf_op jit(solution)/shard_map/all_to_all | solution.py:99
  299.8 26.3 %fusion.15 = f32[2,32,256,256]{3,1,2,0:T(8,128)} fusion(f32[2,32,256,256]{3,2,1,0:T(8,128)} %bitcast.174, f32[1,32,2,32]{3,1,2,0:T(8,128)S(1)} %get-tuple-element.27, f32[1,32,2,32]{3,1,2,0:T(8,128)S(1)} %get-tuple-element.26), kind=kOutput, calls=%fused_computation.27 | convolution fusion | flops 1610616832 | bytes 33570816 | tf_op jit(solution)/shard_map/aibq,bqpc->aipc/dot_general | solution.py:76
  326.1 13.7 %multiply_subtract_fusion.3 = (f32[1,32,256,256]{3,1,2,0:T(8,128)}, f32[1,32,256,256]{3,1,2,0:T(8,128)}) fusion(f32[2,32,256,256]{3,1,2,0:T(8,128)} %fusion.15, f32[32,256]{0,1:T(8,128)S(1)} %copy-done.3, f32[32,256]{0,1:T(8,128)S(1)} %get-tuple-element.42), kind=kLoop, calls=%fused_computation.26 | loop fusion | flops 12582912 | bytes 33619968 | tf_op jit(solution)/shard_map/sub | solution.py:20
  339.8 6.6 pad_maximum_fusion
  346.4 42.2 %convolution_bitcast_fusion.1 = f32[2,512,32,256]{3,1,2,0:T(8,128)} fusion(f32[2,32,256,256]{3,1,2,0:T(8,128)S(1)} %pad_maximum_fusion, f32[1,512,2,256]{3,1,2,0:T(8,128)S(1)} %get-tuple-element.19, f32[1,512,2,256]{3,1,2,0:T(8,128)S(1)} %get-tuple-element.18), kind=kOutput, calls=%fused_computation.7 | convolution fusion | flops 25770328064 | bytes 52428800 | tf_op jit(solution)/shard_map/agbp,bipc->agic/dot_general | solution.py:76
  388.6 22.0 %multiply_subtract_fusion.1 = (f32[1,512,32,256]{3,1,2,0:T(8,128)}, f32[1,512,32,256]{3,1,2,0:T(8,128)}) fusion(f32[2,512,32,256]{3,1,2,0:T(8,128)} %convolution_bitcast_fusion.1, f32[512,256]{1,0:T(8,128)S(1)} %get-tuple-element.29, f32[512,256]{1,0:T(8,128)S(1)} %get-tuple-element.30), kind=kLoop, calls=%fused_computation.21 | loop fusion | flops 25165824 | bytes 68157440 | tf_op jit(solution)/shard_map/sub | solution.py:20
  410.6 22.8 %fusion.22 = f32[512,2,32,32]{0,3,1,2:T(8,128)} fusion(f32[1,32,2,256]{3,1,2,0:T(8,128)S(1)} %get-tuple-element.21, f32[1,32,2,256]{3,1,2,0:T(8,128)S(1)} %get-tuple-element.20, f32[1,512,32,256]{3,1,2,0:T(8,128)} %get-tuple-element.11, f32[1,512,32,256]{3,1,2,0:T(8,128)} %get-tuple-element.10), kind=kOutput, calls=%fused_computation.31 | convolution fusion | flops 3230695424 | bytes 37879808 | tf_op jit(solution)/shard_map/ajbc,bgic->gaij/dot_general | solution.py:76
  433.4 5.0 copy.100
  438.5 5.4 copy.167
  444.3 143.5 %reduce-scatter.4.cloned.1.call-done = f32[16,2048]{1,0:T(8,128)} async-done(((f32[512,2048]{1,0:T(8,128)}), f32[16,2048]{1,0:T(8,128)}) %reduce-scatter.4.cloned.1.call-update) | async-done | bytes 131088
  587.8 2.2 copy.168
  590.1 2.3 fusion.282
  592.3 1.4 copy.170
  593.7 1.4 copy.169
  595.1 0.4 fusion.87
  595.5 0.4 fusion.91
  596.0 0.4 fusion.38
  596.4 0.6 fusion.168
  597.0 0.6 fusion.154
  597.6 0.4 fusion.37
  598.1 0.6 fusion.36
  598.7 0.6 fusion.35
  599.3 2.3 fusion.51
  601.6 2.3 fusion.49
  603.8 2.3 convolution_subtract_fusion.3
  606.1 3.8 fusion.80
  609.9 0.7 compare_select_fusion.1
  610.6 3.1 fusion.48
  613.7 3.1 fusion.70
  616.9 3.1 convolution_subtract_fusion.2
  620.0 3.1 convolution_add_fusion.2
  623.1 1.6 fusion.160
  624.7 1.8 fusion.164
  626.5 1.6 fusion.34
  628.2 0.6 fusion.162
  628.8 0.6 fusion.149
  629.4 1.6 fusion.33
  631.0 0.6 fusion.32
  631.6 0.6 fusion.30
  632.3 0.9 reshape.563
  633.2 1.1 fusion.135
  634.4 57.8 %all-gather.2.cloned.1.call-done = f32[512,2048]{1,0:T(8,128)} async-done(((f32[16,2048]{1,0:T(8,128)}), f32[512,2048]{1,0:T(8,128)}) %all-gather.2.cloned.1.call-update) | async-done | bytes 4194320 | tf_op jit(solution)/shard_map/all_gather | solution.py:130
  692.2 5.3 copy.117
  697.5 20.8 %convolution_bitcast_fusion = f32[2,512,32,256]{3,1,2,0:T(8,128)} fusion(f32[512,2,32,32]{0,3,2,1:T(8,128)} %bitcast.179, f32[1,32,2,256]{3,1,2,0:T(8,128)} %copy-done.2, f32[1,32,2,256]{3,1,2,0:T(8,128)S(1)} %get-tuple-element.20), kind=kOutput, calls=%fused_computation.6 | convolution fusion | flops 3221258240 | bytes 37879808 | tf_op jit(solution)/shard_map/ajbc,gaij->bgic/dot_general | solution.py:76
  718.3 17.2 %multiply_subtract_fusion = (f32[1,512,32,256]{3,1,2,0:T(8,128)S(1)}, f32[1,512,32,256]{3,1,2,0:T(8,128)}) fusion(f32[2,512,32,256]{3,1,2,0:T(8,128)} %convolution_bitcast_fusion, f32[512,256]{1,0:T(8,128)} %get-tuple-element.28, f32[512,256]{1,0:T(8,128)S(1)} %get-tuple-element.30), kind=kLoop, calls=%fused_computation.19 | loop fusion | flops 25165824 | bytes 68157440 | tf_op jit(solution)/shard_map/sub | solution.py:20
  735.5 32.3 %fusion.12 = f32[32,256,2,256]{3,1,2,0:T(8,128)} fusion(f32[1,512,32,256]{3,1,2,0:T(8,128)} %get-tuple-element.9, f32[1,512,32,256]{3,1,2,0:T(8,128)S(1)} %get-tuple-element.8, f32[1,512,2,256]{3,1,2,0:T(8,128)S(1)} %get-tuple-element.19, f32[1,512,2,256]{3,1,2,0:T(8,128)S(1)} %get-tuple-element.18), kind=kOutput, calls=%fused_computation.22 | convolution fusion | flops 25778716672 | bytes 52428800 | tf_op jit(solution)/shard_map/agbp,agic->bipc/dot_general | solution.py:76
  767.8 20.2 %copy.123 = f32[32,256,2,256]{1,0,3,2:T(8,128)} copy(f32[32,256,2,256]{3,1,2,0:T(8,128)} %fusion.12) | data formatting | bytes 33554432 | tf_op jit(solution)/shard_map/agbp,agic->bipc/dot_general | solution.py:76
  788.1 9.8 multiply_subtract_fusion.2
  797.9 13.8 %fusion.18 = f32[2,32,256,256]{3,1,2,0:T(8,128)} fusion(f32[1,32,256,256]{3,1,2,0:T(8,128)} %get-tuple-element.13, f32[1,32,256,256]{3,1,2,0:T(8,128)S(1)} %get-tuple-element.12, f32[1,32,2,32]{3,1,2,0:T(8,128)S(1)} %copy-done.8, f32[1,32,2,32]{3,1,2,0:T(8,128)S(1)} %copy-done.6), kind=kOutput, calls=%fused_computation.28 | convolution fusion | flops 1619005440 | bytes 33570816 | tf_op jit(solution)/shard_map/aibq,aipc->bqpc/dot_general | solution.py:76
  811.7 15.5 %copy.126 = f32[2,32,256,256]{3,2,1,0:T(8,128)S(1)} copy(f32[2,32,256,256]{3,1,2,0:T(8,128)} %fusion.18) | data formatting | bytes 33554432 | tf_op jit(solution)/shard_map/aibq,aipc->bqpc/dot_general | solution.py:76
  827.2 46.1 %copy.127 = f32[2,8192,256]{2,0,1:T(2,128)} copy(f32[2,8192,256]{2,1,0:T(8,128)S(1)} %bitcast.176) | data formatting | bytes 33554432 | tf_op jit(solution)/shard_map/reshape | solution.py:138
  873.3 7.0 all-to-all-start.1
  880.3 0.6 pad_maximum_fusion.5
  880.9 182.4 %all-to-all-done.1 = f32[2,8192,256]{2,0,1:T(2,128)} async-done(((f32[2,8192,256]{2,0,1:T(2,128)}), f32[2,8192,256]{2,0,1:T(2,128)}, u32[]{:S(2)}, u32[]{:S(2)}) %all-to-all-start.1) | async-done | bytes 16777248 | tf_op jit(solution)/shard_map/all_to_all | solution.py:137
  1063.3 12.8 %copy.128 = f32[2,8192,256]{2,1,0:T(8,128)} copy(f32[2,8192,256]{2,0,1:T(2,128)} %all-to-all-done.1) | data formatting | bytes 33554432 | tf_op jit(solution)/shard_map/all_to_all | solution.py:137
  1076.2 16.4 %copy.129 = f32[2,2048,4,256]{1,3,2,0:T(8,128)} copy(f32[2,2048,4,256]{3,1,2,0:T(8,128)} %bitcast.177) | data formatting | bytes 33554432 | tf_op jit(solution)/shard_map/all_to_all | solution.py:137
  1092.6 18.0 %copy.130 = f32[2,2048,1024]{2,1,0:T(8,128)} copy(f32[2,2048,1024]{1,2,0:T(8,128)} %bitcast.178) | data formatting | bytes 33554432
  (53 shorter events, 1.2 us)
Async XLA Ops:
  32.4 7.2 copy-start.12
  32.4 7.2 copy-start.13
  32.5 233.1 %all-to-all-start = ((f32[2,2048,1024]{1,0,2:T(2,128)}), f32[2,2048,1024]{1,0,2:T(2,128)}, u32[]{:S(2)}, u32[]{:S(2)}) async-start(f32[2,2048,1024]{1,0,2:T(2,128)} %copy.94), calls=%async_computation | async-start | bytes 33554432 | tf_op jit(solution)/shard_map/all_to_all | solution.py:99
  39.6 548.3 %reduce-scatter.4.cloned.1.call-start = ((), (), s32[]{:S(2)}) async-start(), calls=%async_computation.4 | async-start | bytes 4325376
  258.6 41.1 %copy-start.5 = (f32[1,32,2,32]{3,1,2,0:T(8,128)}, f32[1,32,2,32]{3,1,2,0:T(8,128)S(1)}, u32[]{:S(2)}) copy-start(f32[1,32,2,32]{3,1,2,0:T(8,128)S(1)} %get-tuple-element.26) | copy-start | bytes 24580
  258.7 41.1 %copy-start.7 = (f32[1,32,2,32]{3,1,2,0:T(8,128)}, f32[1,32,2,32]{3,1,2,0:T(8,128)S(1)}, u32[]{:S(2)}) copy-start(f32[1,32,2,32]{3,1,2,0:T(8,128)S(1)} %get-tuple-element.27) | copy-start | bytes 24580
  258.8 151.8 %copy-start.2 = (f32[1,32,2,256]{3,1,2,0:T(8,128)}, f32[1,32,2,256]{3,1,2,0:T(8,128)S(1)}, u32[]{:S(2)}) copy-start(f32[1,32,2,256]{3,1,2,0:T(8,128)S(1)} %get-tuple-element.21) | copy-start | bytes 196612
  260.0 66.0 %copy-start = (f32[32,256]{0,1:T(8,128)}, f32[32,256]{0,1:T(8,128)S(1)}, u32[]{:S(2)}) copy-start(f32[32,256]{0,1:T(8,128)S(1)} %get-tuple-element.42) | copy-start | bytes 98308
  299.8 26.3 %copy-start.3 = (f32[32,256]{0,1:T(8,128)S(1)}, f32[32,256]{0,1:T(8,128)}, u32[]{:S(2)}) copy-start(f32[32,256]{0,1:T(8,128)} %get-tuple-element.41) | copy-start | bytes 98308
  433.4 10.8 copy-start.14
  433.4 10.9 copy-start.10
  433.4 176.4 %copy-start.9 = (f32[16,2,128]{2,1,0:T(2,128)S(1)}, f32[16,2,128]{2,1,0:T(2,128)}, u32[]{:S(2)}) copy-start(f32[16,2,128]{2,1,0:T(2,128)} %param.9) | copy-start | bytes 49156
  443.9 248.3 %all-gather.2.cloned.1.call-start = ((), (), s32[]{:S(2)}) async-start(), calls=%async_computation.3 | async-start | bytes 4325376 | tf_op jit(solution)/shard_map/all_gather | solution.py:130
  444.2 165.7 %copy-start.11 = (f32[32]{0:T(128)}, f32[32]{0:T(128)S(1)}, u32[]{:S(2)}) copy-start(f32[32]{0:T(128)S(1)} %fusion.207) | copy-start | bytes 388
  767.8 20.2 %copy-start.1 = (f32[32,256]{0,1:T(8,128)S(1)}, f32[32,256]{0,1:T(8,128)}, u32[]{:S(2)}) copy-start(f32[32,256]{0,1:T(8,128)} %copy-done) | copy-start | bytes 98308
  767.8 20.2 %copy-start.4 = (f32[32,256]{0,1:T(8,128)S(1)}, f32[32,256]{0,1:T(8,128)}, u32[]{:S(2)}) copy-start(f32[32,256]{0,1:T(8,128)} %fusion.135) | copy-start | bytes 98308
  788.1 9.8 copy-start.6
  788.1 9.8 copy-start.8
  873.3 190.0 %all-to-all-start.1 = ((f32[2,8192,256]{2,0,1:T(2,128)}), f32[2,8192,256]{2,0,1:T(2,128)}, u32[]{:S(2)}, u32[]{:S(2)}) async-start(f32[2,8192,256]{2,0,1:T(2,128)} %copy.127), calls=%async_computation.1 | async-start | bytes 33554432 | tf_op jit(solution)/shard_map/all_to_all | solution.py:137
Sparse Core Ops, SparseCore 0:
  444.0 143.7 reduce-scatter.3
  633.3 58.8 all-gather.1
where the time goes:
time: 1130 us; the launch traced here: 1120 us
  waiting for transfers between devices  384 us (34%)
  blocking collectives  219 us (19%)
  local copies, waits for them, and re-layouts  213 us (19%)
  matrix products  194 us (17%)
  other arithmetic  79.1 us (7%)
  between operations  14.9 us (1%)
  starting transfers between devices  14.4 us (1%)
    unnamed x1, blocking collectives  219 us
    all_to_all x1, waiting for transfers between devices, per_device(): lax.all_to_all(rows.reshape(2, extent, cols), 'slab', split_axis=1, conca...  182 us
    dot_general x6, matrix products, product_high(): return jnp.einsum(form, left, right, precision=lax.Precision.HIGH)  158 us
    unnamed x3, waiting for transfers between devices  144 us
    sub x4, other arithmetic, complex_mul(): left[0] * right[0] - left[1] * right[1]  62.7 us
    all_gather x1, waiting for transfers between devices, per_device(): lax.all_gather(contrib.reshape(sub_count, 2 * SUB * SUB), both, axis=0, t...  57.8 us
    unnamed x37, local copies, waits for them, and re-layouts  53.7 us
    reshape x1, local copies, waits for them, and re-layouts, per_device(): rows.reshape(2, extent, cols)  46.1 us
  transfers between devices with their start and end apart: 4, of which 3 were waited for; matrix products, arithmetic and copies ran while one was open for 1% of the time, Pallas kernels for 0%

commit v1 on v0

--- a/solution.py
+++ b/solution.py
@@ -134,9 +134,10 @@
     back = product_high("agbp,agic->bipc", real_form(pick_u), spread)
     back = twist(lift_fine(conj(fine)), back) / extent
     rows = product_high("aibq,aipc->bqpc", real_form(coarse), back)
-    residual_image = lax.all_to_all(
-        rows.reshape(2, extent, cols), "slab", split_axis=1, concat_axis=2, tiled=True
-    )
+    own = rows.reshape(2, extent, cols)
+    cells = jnp.split(own, lax.axis_size("slab"), axis=1)
+    received = lax.all_to_all(jnp.stack(cells), "slab", 0, 0)
+    residual_image = jnp.concatenate(received, axis=2)
     return (residual_image, residual_vis)
 
 

time: 1130 us -> 1080 us (0.956)
  local copies, waits for them, and re-layouts: 213 us -> 158 us
    reshape x1, local copies, waits for them, and re-layouts: 46.1 us -> 16.5 us  [per_device(): residual_image = jnp.concatenate(received, axis=2)]
    all_to_all x2 -> x0, local copies, waits for them, and re-layouts: 29.3 us -> none  [per_device(): lax.all_to_all(rows.reshape(2, extent, cols), 'slab', split_axis=1, conca...]
where the time goes in v1:
time: 1080 us; the launch traced here: 1070 us
  waiting for transfers between devices  385 us (36%)
  blocking collectives  219 us (20%)
  matrix products  194 us (18%)
  local copies, waits for them, and re-layouts  158 us (15%)
  other arithmetic  89.7 us (8%)
  between operations  14.9 us (1%)
  starting transfers between devices  14.4 us (1%)
    unnamed x1, blocking collectives  219 us
    all_to_all x1, waiting for transfers between devices, per_device(): received = lax.all_to_all(jnp.stack(cells), 'slab', 0, 0)  182 us
    dot_general x6, matrix products, product_high(): return jnp.einsum(form, left, right, precision=lax.Precision.HIGH)  158 us
    unnamed x3, waiting for transfers between devices  144 us
    sub x4, other arithmetic, complex_mul(): left[0] * right[0] - left[1] * right[1]  62.6 us
    all_gather x1, waiting for transfers between devices, per_device(): lax.all_gather(contrib.reshape(sub_count, 2 * SUB * SUB), both, axis=0, t...  58.5 us
    unnamed x37, local copies, waits for them, and re-layouts  53.7 us
    dot_general x24, matrix products, complex_einsum(): jnp.einsum(form, first, second, precision=lax.Precision.HIGHEST)  36.2 us
  transfers between devices with their start and end apart: 4, of which 3 were waited for; matrix products, arithmetic and copies ran while one was open for 1% of the time, Pallas kernels for 0%

profile of v1, /device:TPU:0, one launch (start us, length us, event | category | flops | bytes accessed | tf_op | source)
XLA Modules:
  0.0 1075.0 jit_solution(18249855540050834867)
XLA Ops:
  7.2 25.3 %copy.97 = f32[2,2048,1024]{1,0,2:T(2,128)} copy(f32[2,2048,1024]{2,1,0:T(8,128)} %param.7) | data formatting | bytes 33554432 | tf_op args[0]
  32.5 7.1 all-to-all-start
  39.8 218.7 %all-reduce = s32[512]{0:T(512)S(1)} all-reduce(s32[512]{0:T(512)S(1)} %fusion.206), channel_id=1, replica_groups=mesh['slab'=4,'bl'=8] {'slab','bl'}, use_global_device_ids=true, to_apply=%add | all-reduce | flops 512 | bytes 4096
  258.9 1.2 sine_multiply_fusion.2
  260.1 2.1 fusion.95
  262.4 3.1 fusion.96
  265.5 17.7 %copy.98 = f32[2,2048,1024]{1,2,0:T(8,128)} copy(f32[2,2048,1024]{1,0,2:T(2,128)} %all-to-all-done) | data formatting | bytes 33554432 | tf_op jit(solution)/shard_map/all_to_all | solution.py:99
  283.3 16.5 %copy.99 = f32[2,4,2048,256]{3,2,1,0:T(8,128)} copy(f32[2,4,2048,256]{2,3,1,0:T(8,128)} %bitcast.182) | data formatting | bytes 33554432 | tf_op jit(solution)/shard_map/all_to_all | solution.py:99
  299.8 26.3 %fusion.15 = f32[2,32,256,256]{3,1,2,0:T(8,128)} fusion(f32[2,32,256,256]{3,2,1,0:T(8,128)} %bitcast.181, f32[1,32,2,32]{3,1,2,0:T(8,128)S(1)} %get-tuple-element.31, f32[1,32,2,32]{3,1,2,0:T(8,128)S(1)} %get-tuple-element.30), kind=kOutput, calls=%fused_computation.28 | convolution fusion | flops 1610616832 | bytes 33570816 | tf_op jit(solution)/shard_map/aibq,bqpc->aipc/dot_general | solution.py:76
  326.1 13.7 %multiply_subtract_fusion.3 = (f32[1,32,256,256]{3,1,2,0:T(8,128)}, f32[1,32,256,256]{3,1,2,0:T(8,128)}) fusion(f32[2,32,256,256]{3,1,2,0:T(8,128)} %fusion.15, f32[32,256]{0,1:T(8,128)S(1)} %copy-done.3, f32[32,256]{0,1:T(8,128)S(1)} %get-tuple-element.46), kind=kLoop, calls=%fused_computation.27 | loop fusion | flops 12582912 | bytes 33619968 | tf_op jit(solution)/shard_map/sub | solution.py:20
  339.8 6.6 pad_maximum_fusion
  346.4 42.3 %convolution_bitcast_fusion.1 = f32[2,512,32,256]{3,1,2,0:T(8,128)} fusion(f32[2,32,256,256]{3,1,2,0:T(8,128)S(1)} %pad_maximum_fusion, f32[1,512,2,256]{3,1,2,0:T(8,128)S(1)} %get-tuple-element.23, f32[1,512,2,256]{3,1,2,0:T(8,128)S(1)} %get-tuple-element.22), kind=kOutput, calls=%fused_computation.7 | convolution fusion | flops 25770328064 | bytes 52428800 | tf_op jit(solution)/shard_map/agbp,bipc->agic/dot_general | solution.py:76
  388.7 21.9 %multiply_subtract_fusion.1 = (f32[1,512,32,256]{3,1,2,0:T(8,128)}, f32[1,512,32,256]{3,1,2,0:T(8,128)}) fusion(f32[2,512,32,256]{3,1,2,0:T(8,128)} %convolution_bitcast_fusion.1, f32[512,256]{1,0:T(8,128)S(1)} %get-tuple-element.33, f32[512,256]{1,0:T(8,128)S(1)} %get-tuple-element.34), kind=kLoop, calls=%fused_computation.22 | loop fusion | flops 25165824 | bytes 68157440 | tf_op jit(solution)/shard_map/sub | solution.py:20
  410.6 22.8 %fusion.22 = f32[512,2,32,32]{0,3,1,2:T(8,128)} fusion(f32[1,32,2,256]{3,1,2,0:T(8,128)S(1)} %get-tuple-element.25, f32[1,32,2,256]{3,1,2,0:T(8,128)S(1)} %get-tuple-element.24, f32[1,512,32,256]{3,1,2,0:T(8,128)} %get-tuple-element.11, f32[1,512,32,256]{3,1,2,0:T(8,128)} %get-tuple-element.10), kind=kOutput, calls=%fused_computation.36 | convolution fusion | flops 3230695424 | bytes 37879808 | tf_op jit(solution)/shard_map/ajbc,bgic->gaij/dot_general | solution.py:76
  433.4 5.0 copy.103
  438.4 5.4 copy.168
  444.3 143.6 %reduce-scatter.4.cloned.1.call-done = f32[16,2048]{1,0:T(8,128)} async-done(((f32[512,2048]{1,0:T(8,128)}), f32[16,2048]{1,0:T(8,128)}) %reduce-scatter.4.cloned.1.call-update) | async-done | bytes 131088
  587.9 2.2 copy.169
  590.1 2.3 fusion.282
  592.3 1.4 copy.171
  593.7 1.4 copy.170
  595.1 0.4 fusion.87
  595.6 0.4 fusion.91
  596.0 0.4 fusion.38
  596.5 0.6 fusion.168
  597.1 0.6 fusion.154
  597.7 0.4 fusion.37
  598.1 0.6 fusion.36
  598.7 0.6 fusion.35
  599.3 2.3 fusion.51
  601.6 2.3 fusion.49
  603.8 2.3 convolution_subtract_fusion.3
  606.1 3.8 fusion.80
  609.9 0.7 compare_select_fusion.1
  610.6 3.1 fusion.48
  613.8 3.1 fusion.70
  616.9 3.1 convolution_subtract_fusion.2
  620.0 3.1 convolution_add_fusion.2
  623.2 1.6 fusion.160
  624.8 1.8 fusion.164
  626.6 1.6 fusion.34
  628.2 0.6 fusion.162
  628.8 0.6 fusion.149
  629.4 1.6 fusion.33
  631.0 0.6 fusion.32
  631.6 0.6 fusion.30
  632.3 0.9 reshape.569
  633.3 1.1 fusion.135
  634.4 58.5 %all-gather.2.cloned.1.call-done = f32[512,2048]{1,0:T(8,128)} async-done(((f32[16,2048]{1,0:T(8,128)}), f32[512,2048]{1,0:T(8,128)}) %all-gather.2.cloned.1.call-update) | async-done | bytes 4194320 | tf_op jit(solution)/shard_map/all_gather | solution.py:130
  692.9 5.3 copy.120
  698.2 20.8 %convolution_bitcast_fusion = f32[2,512,32,256]{3,1,2,0:T(8,128)} fusion(f32[512,2,32,32]{0,3,2,1:T(8,128)} %bitcast.184, f32[1,32,2,256]{3,1,2,0:T(8,128)} %copy-done.2, f32[1,32,2,256]{3,1,2,0:T(8,128)S(1)} %get-tuple-element.24), kind=kOutput, calls=%fused_computation.6 | convolution fusion | flops 3221258240 | bytes 37879808 | tf_op jit(solution)/shard_map/ajbc,gaij->bgic/dot_general | solution.py:76
  719.0 17.2 %multiply_subtract_fusion = (f32[1,512,32,256]{3,1,2,0:T(8,128)S(1)}, f32[1,512,32,256]{3,1,2,0:T(8,128)}) fusion(f32[2,512,32,256]{3,1,2,0:T(8,128)} %convolution_bitcast_fusion, f32[512,256]{1,0:T(8,128)} %get-tuple-element.32, f32[512,256]{1,0:T(8,128)S(1)} %get-tuple-element.34), kind=kLoop, calls=%fused_computation.20 | loop fusion | flops 25165824 | bytes 68157440 | tf_op jit(solution)/shard_map/sub | solution.py:20
  736.2 32.2 %fusion.12 = f32[32,256,2,256]{3,1,2,0:T(8,128)} fusion(f32[1,512,32,256]{3,1,2,0:T(8,128)} %get-tuple-element.9, f32[1,512,32,256]{3,1,2,0:T(8,128)S(1)} %get-tuple-element.8, f32[1,512,2,256]{3,1,2,0:T(8,128)S(1)} %get-tuple-element.23, f32[1,512,2,256]{3,1,2,0:T(8,128)S(1)} %get-tuple-element.22), kind=kOutput, calls=%fused_computation.23 | convolution fusion | flops 25778716672 | bytes 52428800 | tf_op jit(solution)/shard_map/agbp,agic->bipc/dot_general | solution.py:76
  768.4 20.2 %copy.126 = f32[32,256,2,256]{1,0,3,2:T(8,128)} copy(f32[32,256,2,256]{3,1,2,0:T(8,128)} %fusion.12) | data formatting | bytes 33554432 | tf_op jit(solution)/shard_map/agbp,agic->bipc/dot_general | solution.py:76
  788.7 9.8 multiply_subtract_fusion.2
  798.5 13.8 %fusion.18 = f32[2,32,256,256]{3,1,2,0:T(8,128)} fusion(f32[1,32,256,256]{3,1,2,0:T(8,128)} %get-tuple-element.13, f32[1,32,256,256]{3,1,2,0:T(8,128)S(1)} %get-tuple-element.12, f32[1,32,2,32]{3,1,2,0:T(8,128)S(1)} %copy-done.8, f32[1,32,2,32]{3,1,2,0:T(8,128)S(1)} %copy-done.6), kind=kOutput, calls=%fused_computation.29 | convolution fusion | flops 1619005440 | bytes 33570816 | tf_op jit(solution)/shard_map/aibq,aipc->bqpc/dot_general | solution.py:76
  812.3 15.5 %copy.129 = f32[2,32,256,256]{3,2,1,0:T(8,128)S(1)} copy(f32[2,32,256,256]{3,1,2,0:T(8,128)} %fusion.18) | data formatting | bytes 33554432 | tf_op jit(solution)/shard_map/aibq,aipc->bqpc/dot_general | solution.py:76
  827.8 4.6 slice_bitcast_fusion.3
  832.5 10.7 pad_maximum_fusion.1
  843.2 7.0 all-to-all-start.1
  850.2 0.6 pad_maximum_fusion.6
  850.8 182.4 %all-to-all-done.1 = f32[4,2,2048,256]{3,2,1,0:T(8,128)} async-done(((f32[4,2,2048,256]{3,2,1,0:T(8,128)}), f32[4,2,2048,256]{3,2,1,0:T(8,128)}, u32[]{:S(2)}, u32[]{:S(2)}) %all-to-all-start.1) | async-done | bytes 16777248 | tf_op jit(solution)/shard_map/all_to_all | solution.py:139
  1033.2 16.5 %copy.130 = f32[2,2048,4,256]{1,3,2,0:T(8,128)} copy(f32[2,2048,4,256]{3,1,0,2:T(8,128)} %bitcast.64) | data formatting | bytes 33554432 | tf_op jit(solution)/shard_map/reshape | solution.py:140
  1049.7 18.0 %copy.131 = f32[2,2048,1024]{2,1,0:T(8,128)} copy(f32[2,2048,1024]{1,2,0:T(8,128)} %bitcast.183) | data formatting | bytes 33554432
  (53 shorter events, 1.2 us)
Async XLA Ops:
  32.4 7.2 copy-start.12
  32.4 7.2 copy-start.13
  32.5 233.1 %all-to-all-start = ((f32[2,2048,1024]{1,0,2:T(2,128)}), f32[2,2048,1024]{1,0,2:T(2,128)}, u32[]{:S(2)}, u32[]{:S(2)}) async-start(f32[2,2048,1024]{1,0,2:T(2,128)} %copy.97), calls=%async_computation | async-start | bytes 33554432 | tf_op jit(solution)/shard_map/all_to_all | solution.py:99
  39.6 548.3 %reduce-scatter.4.cloned.1.call-start = ((), (), s32[]{:S(2)}) async-start(), calls=%async_computation.4 | async-start | bytes 4325376
  258.7 41.1 %copy-start.5 = (f32[1,32,2,32]{3,1,2,0:T(8,128)}, f32[1,32,2,32]{3,1,2,0:T(8,128)S(1)}, u32[]{:S(2)}) copy-start(f32[1,32,2,32]{3,1,2,0:T(8,128)S(1)} %get-tuple-element.30) | copy-start | bytes 24580
  258.7 41.1 %copy-start.7 = (f32[1,32,2,32]{3,1,2,0:T(8,128)}, f32[1,32,2,32]{3,1,2,0:T(8,128)S(1)}, u32[]{:S(2)}) copy-start(f32[1,32,2,32]{3,1,2,0:T(8,128)S(1)} %get-tuple-element.31) | copy-start | bytes 24580
  258.9 151.7 %copy-start.2 = (f32[1,32,2,256]{3,1,2,0:T(8,128)}, f32[1,32,2,256]{3,1,2,0:T(8,128)S(1)}, u32[]{:S(2)}) copy-start(f32[1,32,2,256]{3,1,2,0:T(8,128)S(1)} %get-tuple-element.25) | copy-start | bytes 196612
  260.1 66.0 %copy-start = (f32[32,256]{0,1:T(8,128)}, f32[32,256]{0,1:T(8,128)S(1)}, u32[]{:S(2)}) copy-start(f32[32,256]{0,1:T(8,128)S(1)} %get-tuple-element.46) | copy-start | bytes 98308
  299.8 26.3 %copy-start.3 = (f32[32,256]{0,1:T(8,128)S(1)}, f32[32,256]{0,1:T(8,128)}, u32[]{:S(2)}) copy-start(f32[32,256]{0,1:T(8,128)} %get-tuple-element.45) | copy-start | bytes 98308
  433.4 10.8 %copy-start.14 = (s32[16]{0:T(128)S(1)}, s32[16]{0:T(128)}, u32[]{:S(2)}) copy-start(s32[16]{0:T(128)} %param.12) | copy-start | bytes 196
  433.4 10.9 %copy-start.10 = (f32[16,2,128]{2,1,0:T(2,128)S(1)}, f32[16,2,128]{2,1,0:T(2,128)}, u32[]{:S(2)}) copy-start(f32[16,2,128]{2,1,0:T(2,128)} %param.8) | copy-start | bytes 49156
  433.4 176.5 %copy-start.9 = (f32[16,2,128]{2,1,0:T(2,128)S(1)}, f32[16,2,128]{2,1,0:T(2,128)}, u32[]{:S(2)}) copy-start(f32[16,2,128]{2,1,0:T(2,128)} %param.9) | copy-start | bytes 49156
  443.8 249.0 %all-gather.2.cloned.1.call-start = ((), (), s32[]{:S(2)}) async-start(), calls=%async_computation.3 | async-start | bytes 4325376 | tf_op jit(solution)/shard_map/all_gather | solution.py:130
  444.1 165.7 %copy-start.11 = (f32[32]{0:T(128)}, f32[32]{0:T(128)S(1)}, u32[]{:S(2)}) copy-start(f32[32]{0:T(128)S(1)} %fusion.207) | copy-start | bytes 388
  768.4 20.2 %copy-start.1 = (f32[32,256]{0,1:T(8,128)S(1)}, f32[32,256]{0,1:T(8,128)}, u32[]{:S(2)}) copy-start(f32[32,256]{0,1:T(8,128)} %copy-done) | copy-start | bytes 98308
  768.4 20.2 %copy-start.4 = (f32[32,256]{0,1:T(8,128)S(1)}, f32[32,256]{0,1:T(8,128)}, u32[]{:S(2)}) copy-start(f32[32,256]{0,1:T(8,128)} %fusion.135) | copy-start | bytes 98308
  788.6 9.8 copy-start.6
  788.6 9.8 copy-start.8
  843.2 190.0 %all-to-all-start.1 = ((f32[4,2,2048,256]{3,2,1,0:T(8,128)}), f32[4,2,2048,256]{3,2,1,0:T(8,128)}, u32[]{:S(2)}, u32[]{:S(2)}) async-start(f32[4,2,2048,256]{3,2,1,0:T(8,128)} %pad_maximum_fusion.1), calls=%async_computation.1 | async-start | bytes 33554432 | tf_op jit(solution)/shard_map/all_to_all | solution.py:139
Sparse Core Ops, SparseCore 0:
  444.0 143.8 reduce-scatter.3
  633.4 59.4 all-gather.1
